TPU v7x, 256 devices: a whole 4x4x8 slice. The times are simulated.
256 devices in a mesh: subj: 16 (over z, x_lo), space: 16 (over x_hi, y, core).
Axes of the slice: x: 4 (x_hi: 2, x_lo: 2; x = x_hi * 2 + x_lo), y: 4, z: 8, core: 2. Of those that a mesh axis runs over, the one named last changes fastest.
Arguments:
- template_warped: bfloat16 [32, 256, 256, 256], P('subj', 'space'), may hold values from -6 to 6
- subject_images: bfloat16 [32, 256, 256, 256], P('subj', 'space'), may hold values from -5 to 5.5, as said below
- jacobians: bfloat16 [32, 256, 256, 256], P('subj', 'space'), may hold values from 0.29882812 to 3
- velocity: float32 [256, 256, 256], P('space', 'subj'), may hold values from -6 to 6
Outputs:
- velocity_new: float32 [256, 256, 256], P('space', 'subj')
Inputs may be any that keep to these rules, and one draw needn't show every extreme that they name: `subject_images`: intensities of the subjects' scans.
All inputs are finite; a program needn't handle non-finite values.
Results may differ from a plain program's by a relative error of at most 0.0003.
Values sent between devices are 32-bit elements; how exact they have to be, the bound alone decides.
A program may use at most 128 MiB of HBM per device.

v0:
```python
import math

import jax
import jax.numpy as jnp
from jax import lax
from jax.sharding import Mesh
from jax.sharding import PartitionSpec as P

SUBJ = ("subj_0", "subj_1")


sigma_sq = 0.05
step_size = 0.25
alpha_reach = 16.0
highest = lax.Precision.HIGHEST


def scatter_axes(value, axes, dim):
    if not axes:
        return value
    nearer = lax.psum_scatter(value, axes[0], scatter_dimension=dim, tiled=True)
    return scatter_axes(nearer, axes[1:], dim)


def smoothing_symbol(first, second, third, length):

    def damping(freq):
        turns = (freq % length).astype(jnp.float32)
        return 2.0 - 2.0 * jnp.cos(turns * (2.0 * math.pi / length))

    total = damping(first) + damping(second) + damping(third)
    return 1.0 / (1.0 + alpha_reach * total) ** 2


def phase_tables(length):
    index = jnp.arange(length, dtype=jnp.int32)
    turns = index[:, None] * index[None, :] % length
    angle = turns.astype(jnp.float32) * (2.0 * math.pi / length)
    return (jnp.cos(angle), jnp.sin(angle))


def packed_tables(length):
    half = length // 2
    index = jnp.arange(length, dtype=jnp.int32)
    freq = jnp.where(index <= half, index, index - half)
    turns = index[:, None] * freq[None, :] % length
    angle = turns.astype(jnp.float32) * (2.0 * math.pi / length)
    forward = jnp.where(index[None, :] <= half, jnp.cos(angle), jnp.sin(angle))
    weight = jnp.where((index == 0) | (index == half), 1.0, 2.0) / length
    inverse = jnp.transpose(forward * weight[None, :])
    return (forward, inverse)


def body(template_warped, subject_images, jacobians, velocity):
    length = template_warped.shape[3]
    half = length // 2
    warped = template_warped.astype(jnp.float32)
    slope = (jnp.roll(warped, -1, axis=3) - jnp.roll(warped, 1, axis=3)) * 0.5
    partial_value = jnp.sum(
        jacobians.astype(jnp.float32) * (subject_images.astype(jnp.float32) - warped) * slope,
        axis=0,
    )
    forward_pack, inverse_pack = packed_tables(length)
    packed = jnp.einsum("xyz,zp->xpy", partial_value, forward_pack, precision=highest)
    packed = scatter_axes(packed, SUBJ, 1)
    packed = packed * (2.0 / sigma_sq)
    cosine, sine = phase_tables(length)
    first_table = jnp.stack([cosine, -sine])
    spectra = jnp.einsum("xpy,cyk->ckpx", packed, first_table, precision=highest)
    lines = lax.all_to_all(spectra, "space", split_axis=1, concat_axis=3, tiled=True)
    forward_table = jnp.stack([jnp.stack([cosine, -sine]), jnp.stack([sine, cosine])])
    freq_lines = jnp.einsum("ckpx,cdxw->dkpw", lines, forward_table, precision=highest)
    ky_index = lax.axis_index("space") * lines.shape[1] + jnp.arange(
        lines.shape[1], dtype=jnp.int32
    )
    p_index = lax.axis_index(SUBJ) * lines.shape[2] + jnp.arange(lines.shape[2], dtype=jnp.int32)
    p_freq = jnp.where(p_index <= half, p_index, p_index - half)
    kx_index = jnp.arange(length, dtype=jnp.int32)
    symbol = smoothing_symbol(
        ky_index[:, None, None], p_freq[None, :, None], kx_index[None, None, :], length
    )
    filtered = freq_lines * symbol[None]
    inverse_table = jnp.stack([jnp.stack([cosine, sine]), jnp.stack([-sine, cosine])]) / length
    back_lines = jnp.einsum("ckpw,cdwx->dxpk", filtered, inverse_table, precision=highest)
    columns = lax.all_to_all(back_lines, "space", split_axis=1, concat_axis=3, tiled=True)
    last_table = jnp.stack([cosine, -sine]) / length
    real_field = jnp.einsum("cxpk,cky->xpy", columns, last_table, precision=highest)
    depth_lines = lax.all_to_all(real_field, SUBJ, split_axis=2, concat_axis=1, tiled=True)
    smoothed = jnp.einsum("xpy,pz->xyz", depth_lines, inverse_pack, precision=highest)
    return velocity - step_size * (2.0 * velocity - smoothed)


def solution(mesh):
    finer = Mesh(mesh.devices.reshape(8, 2, mesh.shape["space"]), ("subj_0", "subj_1", "space"))
    in_specs = (
        P(SUBJ, "space", None, None),
        P(SUBJ, "space", None, None),
        P(SUBJ, "space", None, None),
        P("space", SUBJ, None),
    )
    out_specs = P("space", SUBJ, None)
    return jax.shard_map(body, mesh=finer, in_specs=in_specs, out_specs=out_specs, check_vma=False)
```

profile of v0, /device:TPU:2, one launch (start us, length us, event | category | flops | bytes accessed | tf_op | source)
XLA Modules:
  0.0 249.2 jit_solution(9879604860009872818)
XLA Ops:
  6.5 11.1 %fusion.73 = (f32[2,16,256,255]{3,2,1,0:T(8,128)}, f32[2,16,256,255]{3,2,1,0:T(8,128)}) fusion(bf16[2,16,256,256]{3,2,1,0:T(8,128)(2,1)} %param.4), kind=kLoop, calls=%fused_computation.107 | loop fusion | bytes 33423360 | tf_op jit(solution)/shard_map/jit(_roll_static)/slice | solution.py:58
  17.6 4.2 %fusion.72 = (f32[2,16,256,1]{3,2,1,0:T(8,128)}, f32[2,16,256,1]{3,2,1,0:T(8,128)}) fusion(bf16[2,16,256,256]{3,2,1,0:T(8,128)(2,1)S(1)} %copy-done), kind=kLoop, calls=%fused_computation.106 | loop fusion | bytes 131072 | tf_op jit(solution)/shard_map/jit(_roll_static)/slice | solution.py:58
  21.8 16.3 %fusion.2 = f32[16,256,256]{2,1,0:T(8,128)} fusion(f32[2,16,256,1]{3,2,1,0:T(8,128)} %get-tuple-element.6, f32[2,16,256,255]{3,2,1,0:T(8,128)} %get-tuple-element.8, f32[2,16,256,255]{3,2,1,0:T(8,128)} %get-tuple-element.7, f32[2,16,256,1]{3,2,1,0:T(8,128)} %get-tuple-element.5, bf16[2,16,256,256]{3,2,1,0:T(8,128)(2,1)} %param.5, ...), kind=kLoop, calls=%fused_computation.3 | loop fusion | flops 22020096 | bytes 33554432 | tf_op jit(solution)/shard_map/reduce_sum | solution.py:59
  38.2 11.8 %convolution_bitcast_fusion = f32[16,256,256]{2,1,0:T(8,128)} fusion(f32[16,256,256]{2,1,0:T(8,128)} %fusion.2, s32[256]{0:T(256)S(1)} %add_select_fusion.2, pred[256]{0:T(512)(128)(4,1)S(1)} %iota_compare_fusion), kind=kOutput, calls=%fused_computation.4 | convolution fusion | flops 3222208512 | bytes 8389888 | tf_op jit(solution)/shard_map/xyz,zp->xpy/dot_general | solution.py:64
  50.3 58.2 %reduce-scatter.3.cloned.1.call-done = f32[16,32,256]{2,1,0:T(8,128)} async-done(((f32[16,256,256]{2,1,0:T(8,128)}), f32[16,32,256]{2,1,0:T(8,128)}) %reduce-scatter.3.cloned.1.call-update) | async-done | bytes 524304 | tf_op jit(solution)/shard_map/reduce_scatter | solution.py:21
  111.6 16.6 %reduce-scatter.5.cloned.1.call-done = f32[16,16,256]{2,1,0:T(8,128)} async-done(((f32[16,32,256]{2,1,0:T(8,128)}), f32[16,16,256]{2,1,0:T(8,128)}) %reduce-scatter.5.cloned.1.call-update) | async-done | bytes 262160 | tf_op jit(solution)/shard_map/reduce_scatter | solution.py:21
  129.8 4.4 %copy.13 = f32[2,256,16,16]{2,3,0,1:T(8,128)} copy(f32[2,256,16,16]{1,2,3,0:T(8,128)S(1)} %convolution_bitcast_fusion.3) | data formatting | bytes 1048576 | tf_op jit(solution)/shard_map/xpy,cyk->ckpx/transpose | solution.py:69
  134.2 4.2 %reshape.238 = f32[16,1,8192]{2,1,0:T(1,128)} reshape(f32[256,2,16,16]{3,2,1,0:T(8,128)} %bitcast.87) | data formatting | bytes 1048576
  138.4 6.4 %all-to-all-start = ((f32[16,1,8192]{2,1,0:T(1,128)}), f32[16,1,8192]{2,1,0:T(1,128)S(1)}, u32[]{:S(2)}, u32[]{:S(2)}) async-start(f32[16,1,8192]{2,1,0:T(1,128)} %reshape.238), calls=%async_computation.2 | async-start | bytes 1048576 | tf_op jit(solution)/shard_map/all_to_all | solution.py:70
  145.1 12.1 %all-to-all-done = f32[16,1,8192]{2,1,0:T(1,128)S(1)} async-done(((f32[16,1,8192]{2,1,0:T(1,128)}), f32[16,1,8192]{2,1,0:T(1,128)S(1)}, u32[]{:S(2)}, u32[]{:S(2)}) %all-to-all-start) | async-done | bytes 524320 | tf_op jit(solution)/shard_map/all_to_all | solution.py:70
  159.6 2.8 %reshape.239 = f32[256,2,16,16]{3,2,1,0:T(8,128)} reshape(f32[16,8192]{1,0:T(8,128)S(1)} %reduce) | data formatting | bytes 1048576
  162.3 5.6 %copy.14 = f32[2,16,16,16,16]{4,1,3,2,0:T(8,128)} copy(f32[2,16,16,16,16]{3,4,0,2,1:T(8,128)} %bitcast.89) | data formatting | bytes 1048576 | tf_op jit(solution)/shard_map/all_to_all | solution.py:70
  168.0 3.5 %all_to_all.42 = f32[2,16,16,256]{3,2,1,0:T(8,128)S(1)} reshape(f32[2,16,16,16,16]{4,3,2,1,0:T(8,128)} %bitcast.90) | data formatting | bytes 1048576 | tf_op jit(solution)/shard_map/all_to_all | solution.py:70
  173.7 4.4 %copy.18 = f32[2,256,16,16]{2,3,0,1:T(8,128)} copy(f32[2,256,16,16]{1,2,3,0:T(8,128)S(1)} %convolution_bitcast_fusion.1) | data formatting | bytes 1048576 | tf_op jit(solution)/shard_map/ckpw,cdwx->dxpk/transpose | solution.py:84
  178.1 3.5 %reshape.240 = f32[16,1,8192]{2,1,0:T(1,128)S(1)} reshape(f32[256,2,16,16]{3,2,1,0:T(8,128)} %bitcast.88) | data formatting | bytes 1048576
  181.6 15.2 %all_to_all.54 = f32[16,1,8192]{2,1,0:T(1,128)S(1)} all-to-all(f32[16,1,8192]{2,1,0:T(1,128)S(1)} %reshape.240), channel_id=1, replica_groups=mesh['subj_0'=8,'subj_1'=2,'space'=16] {'space'}, dimensions={0} | all-to-all | bytes 1048576 | tf_op jit(solution)/shard_map/all_to_all | solution.py:85
  198.6 2.8 %reshape.241 = f32[256,2,16,16]{3,2,1,0:T(8,128)} reshape(f32[16,8192]{1,0:T(8,128)S(1)} %reduce.1) | data formatting | bytes 1048576
  201.4 5.6 %copy.19 = f32[2,16,16,16,16]{4,1,3,0,2:T(8,128)} copy(f32[2,16,16,16,16]{3,4,0,2,1:T(8,128)} %bitcast.91) | data formatting | bytes 1048576 | tf_op jit(solution)/shard_map/all_to_all | solution.py:85
  207.0 3.5 %all_to_all.46 = f32[2,16,16,256]{3,2,0,1:T(8,128)S(1)} reshape(f32[2,16,16,16,16]{4,3,2,0,1:T(8,128)} %bitcast.92) | data formatting | bytes 1048576 | tf_op jit(solution)/shard_map/all_to_all | solution.py:85
  213.8 8.8 %all-to-all-start.2 = ((f32[16,1,4096]{2,1,0:T(1,128)}), f32[16,1,4096]{2,1,0:T(1,128)S(1)}, u32[]{:S(2)}, u32[]{:S(2)}) async-start(f32[16,1,4096]{2,1,0:T(1,128)} %reshape.242), calls=%async_computation.4 | async-start | bytes 524288 | tf_op jit(solution)/shard_map/all_to_all | solution.py:88
  222.6 10.1 %all-to-all-done.2 = f32[16,1,4096]{2,1,0:T(1,128)S(1)} async-done(((f32[16,1,4096]{2,1,0:T(1,128)}), f32[16,1,4096]{2,1,0:T(1,128)S(1)}, u32[]{:S(2)}, u32[]{:S(2)}) %all-to-all-start.2) | async-done | bytes 262176 | tf_op jit(solution)/shard_map/all_to_all | solution.py:88
  234.7 2.6 %copy.43 = f32[16,16,16,16]{1,2,3,0:T(8,128)} copy(f32[16,16,16,16]{1,0,3,2:T(8,128)S(1)} %bitcast.94) | data formatting | bytes 524288 | tf_op jit(solution)/shard_map/all_to_all | solution.py:88
  237.3 2.4 all_to_all.50
  239.7 2.2 fusion.6
  (31 shorter events, 17.0 us)
Async XLA Ops:
  6.5 101.9 %reduce-scatter.3.cloned.1.call-start = ((), (), s32[]{:S(2)}) async-start(), calls=%async_computation.5 | async-start | bytes 4718592 | tf_op jit(solution)/shard_map/reduce_scatter | solution.py:21
  6.5 11.1 %copy-start = (bf16[2,16,256,256]{3,2,1,0:T(8,128)(2,1)S(1)}, bf16[2,16,256,256]{3,2,1,0:T(8,128)(2,1)}, u32[]{:S(2)}) copy-start(bf16[2,16,256,256]{3,2,1,0:T(8,128)(2,1)} %param.4) | copy-start | bytes 12582916
  50.0 78.2 %reduce-scatter.5.cloned.1.call-start = ((), (), s32[]{:S(2)}) async-start(), calls=%async_computation.6 | async-start | bytes 786432 | tf_op jit(solution)/shard_map/reduce_scatter | solution.py:21
  138.4 18.8 %all-to-all-start = ((f32[16,1,8192]{2,1,0:T(1,128)}), f32[16,1,8192]{2,1,0:T(1,128)S(1)}, u32[]{:S(2)}, u32[]{:S(2)}) async-start(f32[16,1,8192]{2,1,0:T(1,128)} %reshape.238), calls=%async_computation.2 | async-start | bytes 1048576 | tf_op jit(solution)/shard_map/all_to_all | solution.py:70
  167.9 4.7 %copy-start.1 = (f32[1,2,256,256]{3,2,1,0:T(8,128)S(1)}, f32[1,2,256,256]{3,2,1,0:T(8,128)}, u32[]{:S(2)}) copy-start(f32[1,2,256,256]{3,2,1,0:T(8,128)} %get-tuple-element.14) | copy-start | bytes 1572868
  213.8 18.9 %all-to-all-start.2 = ((f32[16,1,4096]{2,1,0:T(1,128)}), f32[16,1,4096]{2,1,0:T(1,128)S(1)}, u32[]{:S(2)}, u32[]{:S(2)}) async-start(f32[16,1,4096]{2,1,0:T(1,128)} %reshape.242), calls=%async_computation.4 | async-start | bytes 524288 | tf_op jit(solution)/shard_map/all_to_all | solution.py:88
  234.0 5.8 %copy-start.2 = (f32[16,16,256]{2,1,0:T(8,128)S(1)}, f32[16,16,256]{2,1,0:T(8,128)}, u32[]{:S(2)}) copy-start(f32[16,16,256]{2,1,0:T(8,128)} %param.7) | copy-start | bytes 786436
Sparse Core Ops, SparseCore 0:
  50.2 58.2 reduce-scatter.2
  111.0 17.2 reduce-scatter.4
where the time goes:
time: 253 us; the launch traced here: 249 us
  waiting for transfers between devices  97 us (38%)
  local copies, waits for them, and re-layouts  64.5 us (25%)
  other arithmetic  24.7 us (10%)
  matrix products  18.3 us (7%)
  starting transfers between devices  15.5 us (6%)
  blocking collectives  15.2 us (6%)
  between operations  14 us (6%)
    reduce_scatter x2, waiting for transfers between devices, scatter_axes(): nearer = lax.psum_scatter(value, axes[0], scatter_dimension=dim, tiled=True)  74.8 us
    reduce_sum x1, other arithmetic, body(): jnp.sum(jacobians.astype(jnp.float32) * (subject_images.astype(jnp.float3...  16.3 us
    unnamed x12, local copies, waits for them, and re-layouts  15.4 us
    slice x2, local copies, waits for them, and re-layouts, body(): slope = (jnp.roll(warped, -1, axis=3) - jnp.roll(warped, 1, axis=3)) * 0.5  15.3 us
    all_to_all x1, blocking collectives, body(): lax.all_to_all(back_lines, 'space', split_axis=1, concat_axis=3, tiled=True)  15.2 us
    all_to_all x1, waiting for transfers between devices, body(): lax.all_to_all(spectra, 'space', split_axis=1, concat_axis=3, tiled=True)  12.1 us
    dot_general x1, matrix products, body(): jnp.einsum('xyz,zp->xpy', partial_value, forward_pack, precision=highest)  11.8 us
    all_to_all x1, waiting for transfers between devices, body(): lax.all_to_all(real_field, SUBJ, split_axis=2, concat_axis=1, tiled=True)  10.1 us
  transfers between devices with their start and end apart: 4, of which 4 were waited for; matrix products, arithmetic and copies ran while one was open for 1% of the time, Pallas kernels for 0%

commit v1 on v0

v1 whole, which is shorter than its diff:
```python
import functools

import jax
import jax.numpy as jnp
import numpy as np
from jax import lax
from jax.experimental import pallas as pl
from jax.experimental.pallas import tpu as pltpu
from jax.sharding import PartitionSpec as P

sigma_sq = 0.05
step_size = 0.25
alpha_reach = 16.0

N = 256
RING = 8
f32 = jnp.float32
bf16 = jnp.bfloat16
MESH = pl.DeviceIdType.MESH


def tables():
    half = N // 2
    index = np.arange(N)
    freq = np.where(index <= half, index, index - half)
    angle = (index[:, None] * freq[None, :] % N) * (2.0 * np.pi / N)
    wave = np.where(index[None, :] <= half, np.cos(angle), np.sin(angle))
    weight = np.where((index == 0) | (index == half), 1.0, 2.0) / N
    basis = wave * np.sqrt(weight)[None, :]
    lam = 2.0 - 2.0 * np.cos(2.0 * np.pi * freq / N)
    s, pp = np.divmod(np.arange(N), 16)
    order = (s // 2) * 32 + (pp // 8) * 16 + (s % 2) * 8 + pp % 8

    def split(a):
        a = jnp.asarray(a, f32)
        hi = a.astype(bf16)
        return hi, (a - hi.astype(f32)).astype(bf16)

    def split_np(a):
        hi = a.astype(np.float32).astype(jnp.bfloat16)
        lo = (a - hi.astype(np.float64)).astype(np.float32).astype(jnp.bfloat16)
        return hi, lo

    stack = []
    for a in (basis.T, basis, basis.T[order]):
        stack.extend(split_np(a))
    return np.stack(stack), lam.astype(np.float32), lam[order].astype(np.float32)


def halves(a):
    hi = a.astype(bf16)
    return hi, (a - hi.astype(f32)).astype(bf16)


def dot3(a, b, dims=((1,), (0,))):
    def one(x, y):
        return lax.dot_general(x, y, (dims, ((), ())), preferred_element_type=f32)

    return one(a[0], b[0]) + (one(a[1], b[0]) + one(a[0], b[1]))


def kernel(
    w_hbm, i_hbm, j_hbm, tab_hbm, lam_smem, lamrow_ref, lamcol_ref, out_ref,
    w_v, i_v, j_v, tab, T, zxr, xzr, xpr, xfr, rt, ys, xr, vs, cr, ws, dr,
    in_sem, tab_sem, zx_s, zx_r, xz_s, xz_r, xp_s, xp_r, xf_s, xf_r,
    b_s, b_r, c_s, c_r, d_s, d_r,
):
    s = lax.axis_index("subj")
    j = lax.axis_index("space")
    z = s // 2
    xlo = s % 2
    partner = s + 1 - 2 * xlo

    def dev(ss, jj):
        return {"subj": ss, "space": jj}

    tab_copy = pltpu.make_async_copy(tab_hbm, tab, tab_sem)
    tab_copy.start()

    def loads(g):
        rows = pl.ds(4 * g, 4)
        return [
            pltpu.make_async_copy(h.at[:, rows], v.at[:, rows], in_sem.at[g, a])
            for a, (h, v) in enumerate(((w_hbm, w_v), (i_hbm, i_v), (j_hbm, j_v)))
        ]

    for g in range(4):
        for c in loads(g):
            c.start()

    barrier = pltpu.get_barrier_semaphore()

    @pl.loop(1, 16)
    def _(i):
        pl.semaphore_signal(barrier, inc=1, device_id=dev((s + i) % 16, j), device_id_type=MESH)
        pl.semaphore_signal(barrier, inc=1, device_id=dev(s, (j + i) % 16), device_id_type=MESH)

    def owner(d, t):
        return (z + 7 - t) % RING if d == 0 else (z + 1 + t) % RING

    def toward(d):
        return (s + 2) % 16 if d == 0 else (s + 14) % 16

    def remote(src, dst, ss, rs, ds, dj):
        return pltpu.make_async_remote_copy(
            src_ref=src, dst_ref=dst, send_sem=ss, recv_sem=rs,
            device_id=dev(ds, dj), device_id_type=MESH,
        )

    def rows(start, size):
        return pl.ds(pl.multiple_of(start, 8), size)

    def t_zx(g, t):
        return T.at[pl.ds(4 * g, 4), rows(32 * owner(g % 2, t), 16), :]

    def t_xz(g, t, side):
        return T.at[pl.ds(4 * g, 4), rows(32 * owner(g % 2, t) + 16 + 8 * side, 8), :]

    def zx_first(g):
        return remote(t_zx(g, 0), zxr.at[0, g], zx_s.at[0, g], zx_r.at[0, g], toward(g % 2), j)

    def zx_next(g, t):
        return remote(zxr.at[t - 1, g], zxr.at[t, g], zx_s.at[t, g], zx_r.at[t, g], toward(g % 2), j)

    def xp(g, t):
        return remote(t_xz(g, t, 1 - xlo), xpr.at[t, g], xp_s.at[t, g], xp_r.at[t, g], partner, j)

    def xz_first(g):
        return remote(xpr.at[0, g], xzr.at[0, g], xz_s.at[0, g], xz_r.at[0, g], toward(g % 2), j)

    def xz_next(g, t):
        return remote(xzr.at[t - 1, g], xzr.at[t, g], xz_s.at[t, g], xz_r.at[t, g], toward(g % 2), j)

    def xf(g):
        return remote(
            zxr.at[6, g, :, rows(8 * (1 - xlo), 8), :], xfr.at[g], xf_s.at[g], xf_r.at[g], partner, j
        )

    for g in range(4):
        for c in loads(g):
            c.wait()
        if g == 0:
            tab_copy.wait()

        @pl.loop(4 * g, 4 * g + 4)
        def _(x):
            total = None
            for sub in range(2):
                w = w_v[sub, x].astype(f32)
                slope = pltpu.roll(w, N - 1, 1) - pltpu.roll(w, 1, 1)
                term = j_v[sub, x].astype(f32) * (i_v[sub, x].astype(f32) - w) * slope
                total = term if total is None else total + term
            T[x] = dot3((tab[0], tab[1]), halves(total), ((1,), (1,)))

        if g == 0:
            pl.semaphore_wait(barrier, 30)
        zx_first(g).start()
        xp(g, 0).start()
        xp(g, 1).start()

    @pl.loop(2, 8)
    def _(t):
        for g in range(4):
            xp(g, t).start()

    def xz_step0():
        for g in range(4):
            xp(g, 0).wait_recv()
            xpr[0, g] += t_xz(g, 0, xlo)[...]
            xz_first(g).start()

    def zx_step(t):
        for g in range(4):
            remote(zxr.at[t - 1, g], zxr.at[t - 1, g], zx_s.at[t - 1, g], zx_r.at[t - 1, g], toward(g % 2), j).wait_recv()
            zxr[t - 1, g] += t_zx(g, t)[...]

    def xz_step(t):
        for g in range(4):
            xp(g, t).wait_recv()
            remote(xzr.at[t - 1, g], xzr.at[t - 1, g], xz_s.at[t - 1, g], xz_r.at[t - 1, g], toward(g % 2), j).wait_recv()
            xzr[t - 1, g] += t_xz(g, t, xlo)[...] + xpr[t, g]

    def zx_full(t):
        for g in range(4):
            remote(zxr.at[t - 1, g], zxr.at[t - 1, g], zx_s.at[t - 1, g], zx_r.at[t - 1, g], toward(g % 2), j).wait_recv()
            zxr[t - 1, g] += t_zx(g, t)[...]
            zx_next(g, t).start()

    def xz_full(t):
        for g in range(4):
            xp(g, t).wait_recv()
            remote(xzr.at[t - 1, g], xzr.at[t - 1, g], xz_s.at[t - 1, g], xz_r.at[t - 1, g], toward(g % 2), j).wait_recv()
            xzr[t - 1, g] += t_xz(g, t, xlo)[...] + xpr[t, g]
            xz_next(g, t).start()

    def put(first, x, value):
        for lh in range(2):
            rt[lh, pl.ds(first + x, 8, stride=16), :] = value[:, 128 * lh:128 * lh + 128]

    zx_full(1)
    xz_step0()

    @pl.loop(2, 7)
    def _(t):
        zx_full(t)
        xz_full(t - 1)

    for g in range(4):
        remote(zxr.at[6, g], zxr.at[6, g], zx_s.at[6, g], zx_r.at[6, g], toward(g % 2), j).wait_recv()
        zxr[6, g] += t_zx(g, 7)[...]
        xf(g).start()
    xz_full(6)
    for g in range(4):
        xf(g).wait_recv()
        mine = zxr[6, g, :, rows(8 * xlo, 8), :] + xfr[g]
        for q in range(4):
            put(0, 4 * g + q, mine[q])
    xz_step(7)
    for g in range(4):
        for q in range(4):
            put(128, 4 * g + q, xzr[6, g, q])

    ys[...] = dot3(halves(jnp.concatenate([rt[0], rt[1]], axis=1)), (tab[2], tab[3])).reshape(16, 16, N)

    def space_copy(src, dst, ss, rs, i):
        to = (j + i) % 16
        return remote(src.at[to], dst.at[j], ss.at[i], rs.at[i], s, to)

    def subj_copy(src, dst, ss, rs, i):
        to = (s + i) % 16
        return remote(src.at[to], dst.at[s], ss.at[i], rs.at[i], to, j)

    def back_copy(src, dst, ss, rs, i):
        to = (j + i) % 16
        return remote(src.at[:, rows(16 * to, 16)], dst.at[:, rows(16 * j, 16)], ss.at[i], rs.at[i], s, to)

    def exchange(make, src, dst, ss, rs, me):
        @pl.loop(1, 16)
        def _(i):
            make(src, dst, ss, rs, i).start()

        if make is back_copy:
            dst[:, rows(16 * me, 16)] = src[:, rows(16 * me, 16)]
        else:
            dst[me] = src[me]

        @pl.loop(1, 16)
        def _(i):
            make(src, dst, ss, rs, i).wait_recv()

    exchange(space_copy, ys, xr, b_s, b_r, j)
    spec = dot3((tab[0], tab[1]), halves(xr[...].reshape(N, N)))
    damp = 1.0 + alpha_reach * (lamrow_ref[...] + lamcol_ref[...] + lam_smem[s * 16 + j])
    spec = spec * ((1.0 / sigma_sq) / (damp * damp))
    back = dot3((tab[2], tab[3]), halves(spec))
    field = dot3(halves(back), (tab[0], tab[1]))
    vs[0] = field[:, :128]
    vs[1] = field[:, 128:]

    exchange(back_copy, vs, cr, c_s, c_r, j)
    lane = lax.broadcasted_iota(jnp.int32, (16, 128), 1)
    parts = []
    for lh in range(2):
        a = [cr[lh, pl.ds(x, 16, stride=16), :] for x in range(16)]
        for b in range(3):
            step = 16 << b
            keep = (lane // step) % 2 == 0
            new = list(a)
            for x in range(16):
                if not x & (1 << b):
                    y = x | (1 << b)
                    new[x] = jnp.where(keep, a[x], pltpu.roll(a[y], step, 1))
                    new[y] = jnp.where(keep, pltpu.roll(a[x], 128 - step, 1), a[y])
            a = new
        parts.append(a)
    for d in range(16):
        for x3 in range(2):
            ws[d, :, 128 * x3:128 * x3 + 128] = parts[d // 8][8 * x3 + d % 8]

    exchange(subj_copy, ws, dr, d_s, d_r, s)
    res = dot3(halves(dr[...].reshape(N, N)), (tab[4], tab[5]), ((0,), (0,)))
    out_ref[...] = res.reshape(16, 16, N)

    @pl.loop(0, 7)
    def _(t):
        for g in range(4):
            remote(zxr.at[t, g], zxr.at[t, g], zx_s.at[t, g], zx_r.at[t, g], toward(g % 2), j).wait_send()
            remote(xzr.at[t, g], xzr.at[t, g], xz_s.at[t, g], xz_r.at[t, g], toward(g % 2), j).wait_send()

    @pl.loop(0, 8)
    def _(t):
        for g in range(4):
            xp(g, t).wait_send()

    for g in range(4):
        xf(g).wait_send()

    @pl.loop(1, 16)
    def _(i):
        space_copy(ys, xr, b_s, b_r, i).wait_send()
        back_copy(vs, cr, c_s, c_r, i).wait_send()
        subj_copy(ws, dr, d_s, d_r, i).wait_send()


def body(template_warped, subject_images, jacobians, velocity):
    stack, lam, lam_order = tables()
    dma = pltpu.SemaphoreType.DMA
    any_spec = pl.BlockSpec(memory_space=pl.ANY)
    vmem = pl.BlockSpec(memory_space=pltpu.VMEM)
    block = pltpu.VMEM((16, 16, N), f32)
    flat = pltpu.VMEM((2, N, 128), f32)
    inp = pltpu.VMEM((2, 16, N, N), bf16)
    smoothed = pl.pallas_call(
        kernel,
        out_shape=jax.ShapeDtypeStruct((16, 16, N), f32),
        in_specs=[any_spec] * 4 + [pl.BlockSpec(memory_space=pltpu.SMEM), vmem, vmem],
        out_specs=vmem,
        scratch_shapes=[
            inp, inp, inp,
            pltpu.VMEM((6, N, N), bf16),
            pltpu.VMEM((16, N, N), f32),
            pltpu.VMEM((7, 4, 4, 16, N), f32),
            pltpu.VMEM((7, 4, 4, 8, N), f32),
            pltpu.VMEM((8, 4, 4, 8, N), f32),
            pltpu.VMEM((4, 4, 8, N), f32),
            flat, block, block, flat, flat, block, block,
            dma((4, 3)), dma,
            dma((7, 4)), dma((7, 4)), dma((7, 4)), dma((7, 4)),
            dma((8, 4)), dma((8, 4)), dma((4,)), dma((4,)),
            dma((16,)), dma((16,)), dma((16,)), dma((16,)), dma((16,)), dma((16,)),
        ],
        compiler_params=pltpu.CompilerParams(
            collective_id=0, has_side_effects=True, vmem_limit_bytes=48 << 20
        ),
        name="force_smooth",
    )(
        template_warped, subject_images, jacobians, jnp.asarray(stack),
        jnp.asarray(lam_order), jnp.asarray(lam)[None, :], jnp.asarray(lam)[:, None],
    )
    return velocity - step_size * (2.0 * velocity - smoothed)


def solution(mesh):
    big = P("subj", "space", None, None)
    out = P("space", "subj", None)
    return jax.shard_map(
        body, mesh=mesh, in_specs=(big, big, big, out), out_specs=out, check_vma=False
    )
```

time: 253 us -> 79.6 us (0.31); the launches traced: 249 us -> 79.4 us
  waiting for transfers between devices: 97 us -> 0 us
  Pallas kernels: 0 us -> 73 us
  local copies, waits for them, and re-layouts: 64.5 us -> 5.58 us
  other arithmetic: 24.7 us -> 0.75 us
  matrix products: 18.3 us -> 0 us
  starting transfers between devices: 15.5 us -> 0 us
  blocking collectives: 15.2 us -> 0 us
  between operations: 14 us -> 0.02 us
    reduce_scatter x2 -> x0, waiting for transfers between devices: 74.8 us -> none  [scatter_axes(): nearer = lax.psum_scatter(value, axes[0], scatter_dimension=dim, tiled=True)]
    pallas_call x0 -> x1, Pallas kernels: none -> 73 us  [body(): pl.pallas_call(kernel, out_shape=jax.ShapeDtypeStruct((16, 16, N), f32),...]
    all_to_all x7 -> x0, local copies, waits for them, and re-layouts: 23.8 us -> none  [the longest x3 9.74 us: body(): lax.all_to_all(spectra, 'space', split_axis=1, concat_axis=3, tiled=True)]
    all_to_all x2 -> x0, waiting for transfers between devices: 22.2 us -> none  [the longest x1 12.1 us: body(): lax.all_to_all(spectra, 'space', split_axis=1, concat_axis=3, tiled=True)]
    dot_general x6 -> x0, matrix products: 18.3 us -> none  [the longest x1 11.8 us: body(): jnp.einsum('xyz,zp->xpy', partial_value, forward_pack, precision=highest)]
    reduce_sum x1 -> x0, other arithmetic: 16.3 us -> none  [body(): jnp.sum(jacobians.astype(jnp.float32) * (subject_images.astype(jnp.float3...]
    slice x2 -> x0, local copies, waits for them, and re-layouts: 15.3 us -> none  [body(): slope = (jnp.roll(warped, -1, axis=3) - jnp.roll(warped, 1, axis=3)) * 0.5]
    all_to_all x2 -> x0, starting transfers between devices: 15.2 us -> none  [the longest x1 8.79 us: body(): lax.all_to_all(real_field, SUBJ, split_axis=2, concat_axis=1, tiled=True)]
  transfers between devices with their start and end apart: 4 -> 0, of which waited for: 4 -> 0; matrix products, arithmetic and copies ran while one was open for 1% -> 0% of each run, Pallas kernels for 0% -> 0%
where the time goes in v1:
time: 79.6 us; the launch traced here: 79.4 us
  Pallas kernels  73 us (92%)
  local copies, waits for them, and re-layouts  5.58 us (7%)
    pallas_call x1, Pallas kernels, body(): pl.pallas_call(kernel, out_shape=jax.ShapeDtypeStruct((16, 16, N), f32),...  73 us
    unnamed x12, local copies, waits for them, and re-layouts  5.58 us

profile of v1, /device:TPU:2, one launch (start us, length us, event | category | flops | bytes accessed | tf_op | source)
XLA Modules:
  0.0 79.4 jit_solution(6504918245242042676)
XLA Ops:
  0.0 0.0 copy-start
  0.0 2.2 %copy-done = bf16[2,16,256,256]{3,2,1,0:T(8,128)(2,1)S(1)} copy-done((bf16[2,16,256,256]{3,2,1,0:T(8,128)(2,1)S(1)}, bf16[2,16,256,256]{3,2,1,0:T(8,128)(2,1)}, u32[]{:S(2)}) %copy-start) | copy-done | bytes 4194328
  2.2 0.0 copy-start.1
  2.2 1.1 %copy-done.1 = bf16[6,256,256]{2,1,0:T(8,128)(2,1)S(1)} copy-done((bf16[6,256,256]{2,1,0:T(8,128)(2,1)S(1)}, bf16[6,256,256]{2,1,0:T(8,128)(2,1)}, u32[]{:S(2)}) %copy-start.1) | copy-done | bytes 786456
  3.3 0.0 copy-start.2
  3.3 0.9 %copy-done.2 = f32[256,1]{1,0:T(8,128)S(1)} copy-done((f32[256,1]{1,0:T(8,128)S(1)}, f32[256,1]{1,0:T(8,128)}, u32[]{:S(2)}) %copy-start.2) | copy-done | bytes 1048
  4.2 0.0 copy-start.3
  4.2 0.7 copy-done.3
  4.9 0.0 copy-start.4
  4.9 0.7 copy-done.4
  5.6 0.0 copy-start.5
  5.6 73.0 %force_smooth.1 = f32[16,16,256]{2,1,0:T(8,128)S(1)} custom-call(bf16[2,16,256,256]{3,2,1,0:T(8,128)(2,1)S(1)} %copy-done, bf16[2,16,256,256]{3,2,1,0:T(8,128)(2,1)} %i_hbm.1, bf16[2,16,256,256]{3,2,1,0:T(8,128)(2,1)} %j_hbm.1, bf16[6,256,256]{2,1,0:T(8,128)(2,1)S(1)} %copy-done.1, f32[256]{0:T(256)S(1)} %copy-done.4, f32[1,256]{1,0:T(1,128)S(1)} %copy-done.3, ...), custom_call_target="tpu_custom_call" | custom-call | tf_op jit(solution)/shard_map/force_smooth/pallas_call | solution.py:313
  78.6 0.0 copy-done.5
  78.6 0.8 multiply_subtract_fusion
Async XLA Ops:
  0.0 2.2 %copy-start = (bf16[2,16,256,256]{3,2,1,0:T(8,128)(2,1)S(1)}, bf16[2,16,256,256]{3,2,1,0:T(8,128)(2,1)}, u32[]{:S(2)}) copy-start(bf16[2,16,256,256]{3,2,1,0:T(8,128)(2,1)} %w_hbm.1) | copy-start | bytes 12582916
  2.2 1.1 %copy-start.1 = (bf16[6,256,256]{2,1,0:T(8,128)(2,1)S(1)}, bf16[6,256,256]{2,1,0:T(8,128)(2,1)}, u32[]{:S(2)}) copy-start(bf16[6,256,256]{2,1,0:T(8,128)(2,1)} %constant.10.clone.tab_hbm) | copy-start | bytes 2359300
  3.3 0.9 %copy-start.2 = (f32[256,1]{1,0:T(8,128)S(1)}, f32[256,1]{1,0:T(8,128)}, u32[]{:S(2)}) copy-start(f32[256,1]{1,0:T(8,128)} %constant.17.lamcol_ref) | copy-start | bytes 3076
  4.2 0.7 copy-start.3
  4.9 0.7 copy-start.4
  5.6 73.0 %copy-start.5 = (f32[16,16,256]{2,1,0:T(8,128)S(1)}, f32[16,16,256]{2,1,0:T(8,128)}, u32[]{:S(2)}) copy-start(f32[16,16,256]{2,1,0:T(8,128)} %param.10) | copy-start | bytes 786436

commit v2 on v1

v2 whole, which is shorter than its diff:
```python
import jax
import jax.numpy as jnp
import numpy as np
from jax import lax
from jax.experimental import pallas as pl
from jax.experimental.pallas import tpu as pltpu
from jax.sharding import PartitionSpec as P

sigma_sq = 0.05
step_size = 0.25
alpha_reach = 16.0

N = 256
RING = 8
f32 = jnp.float32
bf16 = jnp.bfloat16
MESH = pl.DeviceIdType.MESH


ORDER = (
    ("zx", 0, 0, 0), ("zx", 0, 0, 1), ("zx", 0, 1, 0), ("zx", 0, 1, 1), ("zx", 0, 2, 0), ("zx", 0, 2, 1),
    ("xp", 0, 0, 0), ("xp", 1, 1, 0), ("xp", 0, 1, 0), ("xp", 0, 2, 0), ("zx", 1, 0, 0), ("zx", 1, 0, 1),
    ("zx", 0, 3, 0), ("zx", 1, 1, 1), ("xp", 2, 3, 0), ("xp", 0, 3, 0), ("xz", 0, 0, 0), ("xp", 2, 2, 0),
    ("xp", 4, 2, 0), ("xp", 1, 0, 0), ("xp", 1, 2, 0), ("zx", 0, 3, 1), ("zx", 1, 1, 0), ("xp", 1, 3, 0),
    ("xp", 7, 2, 0), ("xz", 0, 1, 1), ("xp", 2, 0, 0), ("xp", 4, 0, 0), ("zx", 1, 2, 0), ("xp", 4, 3, 0),
    ("zx", 2, 0, 0), ("xp", 7, 0, 0), ("zx", 1, 2, 1), ("xp", 2, 1, 0), ("xz", 0, 2, 0), ("xp", 6, 2, 0),
    ("xz", 0, 3, 1), ("xz", 0, 2, 1), ("zx", 2, 1, 1), ("xp", 6, 1, 0), ("zx", 1, 3, 1), ("xz", 1, 0, 0),
    ("xp", 3, 0, 0), ("xp", 3, 2, 0), ("zx", 1, 3, 0), ("zx", 2, 2, 0), ("xz", 0, 3, 0), ("zx", 2, 2, 1),
    ("xz", 1, 2, 0), ("xz", 1, 3, 1), ("xp", 5, 2, 0), ("zx", 3, 0, 0), ("zx", 2, 1, 0), ("xp", 3, 3, 0),
    ("xz", 0, 0, 1), ("zx", 3, 1, 1), ("xz", 0, 1, 0), ("xp", 4, 1, 0), ("xp", 3, 1, 0), ("xp", 5, 1, 0),
    ("xz", 1, 1, 1), ("zx", 2, 3, 1), ("xp", 6, 3, 0), ("xp", 5, 3, 0), ("xz", 2, 0, 0), ("xz", 1, 2, 1),
    ("xz", 2, 3, 1), ("xz", 2, 2, 0), ("xz", 1, 0, 1), ("xp", 6, 0, 0), ("xz", 1, 3, 0), ("xz", 2, 1, 1),
    ("xp", 5, 0, 0), ("xp", 7, 3, 0), ("zx", 2, 0, 1), ("zx", 2, 3, 0), ("xp", 7, 1, 0), ("xz", 1, 1, 0),
    ("zx", 3, 3, 1), ("zf", 0, 1, 0), ("zx", 3, 2, 0), ("xz", 3, 2, 0), ("xz", 2, 0, 1), ("xz", 3, 0, 0),
    ("xz", 2, 3, 0), ("xz", 2, 2, 1), ("xz", 3, 3, 1), ("xz", 3, 1, 1), ("xz", 2, 1, 0), ("zf", 0, 0, 0),
    ("zf", 0, 3, 0), ("zf", 0, 2, 0), ("xf", 0, 2, 0), ("xf", 0, 3, 0), ("xf", 0, 0, 0), ("xf", 0, 1, 0),
)


def tables():
    half = N // 2
    index = np.arange(N)
    freq = np.where(index <= half, index, index - half)
    angle = (index[:, None] * freq[None, :] % N) * (2.0 * np.pi / N)
    wave = np.where(index[None, :] <= half, np.cos(angle), np.sin(angle))
    weight = np.where((index == 0) | (index == half), 1.0, 2.0) / N
    basis = wave * np.sqrt(weight)[None, :]
    lam = 2.0 - 2.0 * np.cos(2.0 * np.pi * freq / N)

    def packed(s, half, q):
        return (s // 2) * 32 + half * 16 + (s % 2) * 8 + q

    s, jj = np.divmod(np.arange(N), 16)
    filtered = packed(s, jj % 2, jj // 2)
    half, s, q = np.arange(N) // 128, np.arange(N) // 8 % 16, np.arange(N) % 8
    gathered = packed(s, half, q)

    def split(a):
        hi = a.astype(np.float32).astype(jnp.bfloat16)
        lo = (a - hi.astype(np.float64)).astype(np.float32).astype(jnp.bfloat16)
        return hi, lo

    stack = []
    for a in (basis.T, basis, basis.T[gathered]):
        stack.extend(split(a))
    shift = np.roll(np.eye(N), 1, axis=0) - np.roll(np.eye(N), -1, axis=0)
    stack.append(shift.astype(jnp.bfloat16))
    damp = 1.0 + alpha_reach * (lam[:, None] + lam[None, :])
    own = np.broadcast_to(alpha_reach * lam[filtered][:, None], (N, 128))
    return np.stack(stack), np.concatenate([damp, own], axis=1).astype(np.float32)


def halves(a):
    hi = a.astype(bf16)
    return hi, (a - hi.astype(f32)).astype(bf16)


def dot3(a, b, dims=((1,), (0,))):
    def one(x, y):
        return lax.dot_general(x, y, (dims, ((), ())), preferred_element_type=f32)

    return one(a[0], b[0]) + (one(a[1], b[0]) + one(a[0], b[1]))


def kernel(
    w_hbm, i_hbm, j_hbm, tab_hbm, damp_hbm, out_ref,
    w_v, i_v, j_v, tab, damp_v, T, zxr, xzr, xpr, rt0, rt1, xr, vs, cr, ws, dr,
    in_sem, tab_sem, damp_sem, zx_s, zx_r, xz_s, xz_r, xp_s, xp_r,
    b0_s, b1_s, b_r, c_s, c_r, d_s, d_r,
):
    s = lax.axis_index("subj")
    j = lax.axis_index("space")
    z = s // 2
    xlo = s % 2
    partner = s + 1 - 2 * xlo

    def dev(ss, jj):
        return {"subj": ss, "space": jj}

    tab_copy = pltpu.make_async_copy(tab_hbm, tab, tab_sem)
    tab_copy.start()

    def loads(g):
        rows = pl.ds(4 * g, 4)
        return [
            pltpu.make_async_copy(h.at[:, rows], v.at[:, rows], in_sem.at[g, a])
            for a, (h, v) in enumerate(((w_hbm, w_v), (i_hbm, i_v), (j_hbm, j_v)))
        ]

    for g in range(4):
        for c in loads(g):
            c.start()
    damp_copy = pltpu.make_async_copy(damp_hbm, damp_v, damp_sem)
    damp_copy.start()

    barrier = pltpu.get_barrier_semaphore()

    @pl.loop(1, 16)
    def _(i):
        pl.semaphore_signal(barrier, inc=1, device_id=dev((s + i) % 16, j), device_id_type=MESH)
        pl.semaphore_signal(barrier, inc=1, device_id=dev(s, (j + i) % 16), device_id_type=MESH)
        pl.semaphore_signal(barrier, inc=1, device_id=dev(partner, (j + i) % 16), device_id_type=MESH)

    def toward(d):
        return (s + 2) % 16 if d == 0 else (s + 14) % 16

    def remote(src, dst, ss, rs, ds, dj):
        return pltpu.make_async_remote_copy(
            src_ref=src, dst_ref=dst, send_sem=ss, recv_sem=rs,
            device_id=dev(ds, dj), device_id_type=MESH,
        )

    def rows(start, size):
        return pl.ds(pl.multiple_of(start, 8), size)

    def hops(g, d):
        return 4 if d == g % 2 else 3

    def owner(d, dist):
        return (z + dist) % RING if d == 0 else (z + RING - dist) % RING

    def t_zx(g, zo):
        return T.at[pl.ds(4 * g, 4), rows(32 * zo, 16), :]

    def t_xz(g, zo, side):
        return T.at[pl.ds(4 * g, 4), rows(32 * zo + 16 + 8 * side, 8), :]

    def piece(d, dist):
        return {4: 0, 3: 1 + d, 2: 3 + d, 1: 5 + d, 0: 7}[dist]

    def piece_owner(k):
        return (z, owner(0, 4), owner(0, 3), owner(1, 3), owner(0, 2), owner(1, 2), owner(0, 1), owner(1, 1))[(k + 1) % 8]

    def xp(g, k):
        return remote(t_xz(g, piece_owner(k), 1 - xlo), xpr.at[k, g], xp_s.at[k, g], xp_r.at[k, g], partner, j)

    def hop(buf, ss, rs, g, d, r, src=None):
        src = buf.at[d, r - 1, g] if src is None else src
        return remote(src, buf.at[d, r, g], ss.at[d, r, g], rs.at[d, r, g], toward(d), j)

    def arrived(buf, ss, rs, g, d, r):
        hop(buf, ss, rs, g, d, r, buf.at[d, r, g]).wait_recv()

    zx = (zxr, zx_s, zx_r)
    xz = (xzr, xz_s, xz_r)

    def zx_send(g, d, r):
        own = t_zx(g, owner(d, hops(g, d) - r))
        if r == 0:
            hop(*zx, g, d, 0, own).start()
        else:
            arrived(*zx, g, d, r - 1)
            zxr[d, r - 1, g] += own[...]
            hop(*zx, g, d, r).start()

    def xz_send(g, d, r):
        dist = hops(g, d) - r
        k = piece(d, dist)
        own = t_xz(g, owner(d, dist), xlo)
        xp(g, k).wait_recv()
        if r == 0:
            xpr[k, g] += own[...]
            hop(*xz, g, d, 0, xpr.at[k, g]).start()
        else:
            arrived(*xz, g, d, r - 1)
            xzr[d, r - 1, g] += own[...] + xpr[k, g]
            hop(*xz, g, d, r).start()

    def put(ref, x, value):
        for lh in range(2):
            ref[lh, pl.ds(x, 8, stride=16), :] = value[:, 128 * lh:128 * lh + 128]

    def last(buf, sems_s, sems_r, g):
        for d in range(2):
            arrived(buf, sems_s, sems_r, g, d, hops(g, d) - 1)
        return buf[0, hops(g, 0) - 1, g] + buf[1, hops(g, 1) - 1, g]

    def zx_last(g):
        total = t_zx(g, z)[...] + last(*zx, g)
        for q in range(4):
            put(rt0.at[0], 4 * g + q, total[q, :8])
            put(rt0.at[1], 4 * g + q, total[q, 8:])

    def xz_last(g):
        xp(g, 7).wait_recv()
        total = t_xz(g, z, xlo)[...] + xpr[7, g] + last(*xz, g)
        for q in range(4):
            put(rt1, 4 * g + q, total[q])

    def to_even(m):
        side, q = m // 8, (m + j // 2) % 8
        return side, q, jnp.logical_and(side == xlo, 2 * q == j)

    def even_copy(side, q):
        return remote(
            rt0.at[side, :, rows(16 * q, 16)], xr.at[xlo, :, rows(16 * j, 16)],
            b0_s.at[side, q], b_r.at[xlo, j], 2 * z + side, 2 * q,
        )

    def odd_copy(q):
        return remote(
            rt1.at[:, rows(16 * q, 16)], xr.at[0, :, rows(16 * j, 16)],
            b1_s.at[q], b_r.at[0, j], s, 2 * q + 1,
        )

    def even_sends():
        @pl.loop(0, 16)
        def _(m):
            side, q, local = to_even(m)

            @pl.when(jnp.logical_not(local))
            def _():
                even_copy(side, q).start()

        @pl.when(j % 2 == 0)
        def _():
            xr[xlo, :, rows(16 * j, 16)] = rt0[xlo, :, rows(8 * j, 16)]

    def odd_sends():
        @pl.loop(0, 8)
        def _(m):
            q = (m + j // 2) % 8

            @pl.when(2 * q + 1 != j)
            def _():
                odd_copy(q).start()

        @pl.when(j % 2 == 1)
        def _():
            xr[0, :, rows(16 * j, 16)] = rt1[:, rows(8 * (j - 1), 16)]

    def compute(g):
        for c in loads(g):
            c.wait()
        if g == 0:
            tab_copy.wait()

        @pl.loop(4 * g, 4 * g + 4)
        def _(x):
            total = None
            for sub in range(2):
                w = w_v[sub, x]
                slope = jnp.dot(w, tab[6], preferred_element_type=f32)
                term = j_v[sub, x].astype(f32) * (i_v[sub, x].astype(f32) - w.astype(f32)) * slope
                total = term if total is None else total + term
            T[x] = dot3((tab[0], tab[1]), halves(total), ((1,), (1,)))

    act = {
        "zx": zx_send, "xz": xz_send, "xp": lambda g, d, k: xp(g, k).start(),
        "zf": lambda g, d, r: zx_last(g), "xf": lambda g, d, r: xz_last(g),
    }
    computed = summed = 0
    for name, r, g, d in ORDER:
        while computed <= g:
            compute(computed)
            if computed == 0:
                pl.semaphore_wait(barrier, 45)
            computed += 1
        act[name](g, d, r)
        summed += name == "zf"
        if name == "zf" and summed == 4:
            even_sends()
    odd_sends()

    def xr_part(side, src):
        part = xr.at[side, :, rows(16 * src, 16)]
        return remote(part, part, b_r.at[side, src], b_r.at[side, src], s, (j + 1) % 16)

    @pl.loop(0, 16)
    def _(src):
        @pl.when(jnp.logical_or(src != j, jnp.logical_and(j % 2 == 0, xlo == 1)))
        def _():
            xr_part(0, src).wait_recv()

        @pl.when(jnp.logical_and(j % 2 == 0, jnp.logical_or(src != j, xlo == 0)))
        def _():
            xr_part(1, src).wait_recv()

    @pl.when(j % 2 == 0)
    def _():
        xr[0] += xr[1]

    lines = dot3(halves(jnp.concatenate([xr[0, 0], xr[0, 1]], axis=1)), (tab[2], tab[3]))
    spec = dot3((tab[0], tab[1]), halves(lines))
    damp_copy.wait()
    own = damp_v[rows(16 * s + 8 * (j // 8), 8), N:]
    own = jnp.sum(jnp.where(lax.broadcasted_iota(jnp.int32, own.shape, 0) == j % 8, own, 0.0), axis=0, keepdims=True)
    damp = damp_v[:, :N] + jnp.concatenate([own, own], axis=1)
    spec = spec * ((1.0 / sigma_sq) / (damp * damp))
    back = dot3((tab[2], tab[3]), halves(spec))
    field = dot3(halves(back), (tab[0], tab[1]))
    vs[0] = field[:, :128]
    vs[1] = field[:, 128:]

    def back_copy(to):
        return remote(
            vs.at[:, rows(16 * to, 16)], cr.at[:, rows(16 * j, 16)], c_s.at[to], c_r.at[j], s, to
        )

    @pl.loop(1, 16)
    def _(i):
        back_copy((j + i) % 16).start()

    cr[:, rows(16 * j, 16)] = vs[:, rows(16 * j, 16)]

    def depth_copy(half, to):
        return remote(
            ws.at[half, to], dr.at[half, s], d_s.at[half, to], d_r.at[half, s], to, j
        )

    lane = lax.broadcasted_iota(jnp.int32, (8, 128), 1)
    for half in range(2):
        @pl.loop(0, 8)
        def _(q):
            src = 2 * q + half

            @pl.when(src != j)
            def _():
                part = cr.at[:, rows(16 * src, 16)]
                remote(part, part, c_s.at[src], c_r.at[src], s, src).wait_recv()

        parts = []
        for lh in range(2):
            a = [cr[lh, pl.ds(16 * half + x, 8, stride=32), :] for x in range(16)]
            for b in range(3):
                step = 16 << b
                keep = (lane // step) % 2 == 0
                new = list(a)
                for x in range(16):
                    if not x & (1 << b):
                        y = x | (1 << b)
                        new[x] = jnp.where(keep, a[x], pltpu.roll(a[y], step, 1))
                        new[y] = jnp.where(keep, pltpu.roll(a[x], 128 - step, 1), a[y])
                a = new
            parts.append(a)
        for d in range(16):
            for x3 in range(2):
                ws[half, d, :, 128 * x3:128 * x3 + 128] = parts[d // 8][8 * x3 + d % 8]

        @pl.loop(1, 16)
        def _(i):
            depth_copy(half, (s + i) % 16).start()

        dr[half, s] = ws[half, s]

    @pl.loop(1, 16)
    def _(i):
        src = (s + i) % 16
        for half in range(2):
            part = dr.at[half, src]
            remote(part, part, d_s.at[half, src], d_r.at[half, src], src, j).wait_recv()

    res = dot3(halves(dr[...].reshape(N, N)), (tab[4], tab[5]), ((0,), (0,)))
    out_ref[...] = res.reshape(16, 16, N)

    for g in range(4):
        for d in range(2):
            for r in range(hops(g, d)):
                hop(*zx, g, d, r, zxr.at[d, r, g]).wait_send()
                hop(*xz, g, d, r, xzr.at[d, r, g]).wait_send()
        for k in range(8):
            xp(g, k).wait_send()

    @pl.loop(0, 16)
    def _(m):
        side, q, local = to_even(m)

        @pl.when(jnp.logical_not(local))
        def _():
            even_copy(side, q).wait_send()

    @pl.loop(0, 8)
    def _(q):
        @pl.when(2 * q + 1 != j)
        def _():
            odd_copy(q).wait_send()

    @pl.loop(1, 16)
    def _(i):
        back_copy((j + i) % 16).wait_send()
        for half in range(2):
            depth_copy(half, (s + i) % 16).wait_send()


def body(template_warped, subject_images, jacobians, velocity):
    stack, damp = tables()
    dma = pltpu.SemaphoreType.DMA
    any_spec = pl.BlockSpec(memory_space=pltpu.HBM)
    vmem = pl.BlockSpec(memory_space=pltpu.VMEM)
    flat = pltpu.VMEM((2, N, 128), f32)
    inp = pltpu.VMEM((2, 16, N, N), bf16)
    smoothed = pl.pallas_call(
        kernel,
        out_shape=jax.ShapeDtypeStruct((16, 16, N), f32),
        in_specs=[any_spec] * 5,
        out_specs=vmem,
        scratch_shapes=[
            inp, inp, inp,
            pltpu.VMEM((7, N, N), bf16),
            pltpu.VMEM((N, N + 128), f32),
            pltpu.VMEM((16, N, N), f32),
            pltpu.VMEM((2, 4, 4, 4, 16, N), f32),
            pltpu.VMEM((2, 4, 4, 4, 8, N), f32),
            pltpu.VMEM((8, 4, 4, 8, N), f32),
            pltpu.VMEM((2, 2, 128, 128), f32),
            pltpu.VMEM((2, 128, 128), f32),
            pltpu.VMEM((2, 2, N, 128), f32),
            flat, flat,
            pltpu.VMEM((2, 16, 8, N), f32),
            pltpu.VMEM((2, 16, 8, N), f32),
            dma((4, 3)), dma, dma,
            dma((2, 4, 4)), dma((2, 4, 4)), dma((2, 4, 4)), dma((2, 4, 4)),
            dma((8, 4)), dma((8, 4)),
            dma((2, 8)), dma((8,)), dma((2, 16)),
            dma((16,)), dma((16,)), dma((2, 16)), dma((2, 16)),
        ],
        compiler_params=pltpu.CompilerParams(
            collective_id=0, has_side_effects=True, vmem_limit_bytes=67043328
        ),
        name="force_smooth",
    )(
        template_warped, subject_images, jacobians, jnp.asarray(stack), jnp.asarray(damp),
    )
    return velocity - step_size * (2.0 * velocity - smoothed)


def solution(mesh):
    big = P("subj", "space", None, None)
    out = P("space", "subj", None)
    return jax.shard_map(
        body, mesh=mesh, in_specs=(big, big, big, out), out_specs=out, check_vma=False
    )
```

time: 79.6 us -> 72.5 us (0.911)
  local copies, waits for them, and re-layouts: 5.58 us -> 0 us
  Pallas kernels: 73 us -> 70.4 us
  other arithmetic: 0.75 us -> 1.78 us
    unnamed x12 -> x0, local copies, waits for them, and re-layouts: 5.58 us -> none
    pallas_call x1, Pallas kernels: 73 us -> 70.4 us  [body(): pl.pallas_call(kernel, out_shape=jax.ShapeDtypeStruct((16, 16, N), f32),...]
    sub x1, other arithmetic: 0.75 us -> 1.78 us  [body(): return velocity - step_size * (2.0 * velocity - smoothed)]
where the time goes in v2:
time: 72.5 us; the launch traced here: 72.2 us
  Pallas kernels  70.4 us (97%)
  other arithmetic  1.78 us (2%)
    pallas_call x1, Pallas kernels, body(): pl.pallas_call(kernel, out_shape=jax.ShapeDtypeStruct((16, 16, N), f32),...  70.4 us
    sub x1, other arithmetic, body(): return velocity - step_size * (2.0 * velocity - smoothed)  1.78 us

profile of v2, /device:TPU:2, one launch (start us, length us, event | category | flops | bytes accessed | tf_op | source)
XLA Modules:
  0.0 72.2 jit_solution(6413760937472025042)
XLA Ops:
  0.0 70.4 %force_smooth.1 = f32[16,16,256]{2,1,0:T(8,128)} custom-call(bf16[2,16,256,256]{3,2,1,0:T(8,128)(2,1)} %w_hbm.1, bf16[2,16,256,256]{3,2,1,0:T(8,128)(2,1)} %i_hbm.1, bf16[2,16,256,256]{3,2,1,0:T(8,128)(2,1)} %j_hbm.1, bf16[7,256,256]{2,1,0:T(8,128)(2,1)} %constant.8.clone.tab_hbm, f32[256,384]{1,0:T(8,128)} %constant.9.clone.damp_hbm), custom_call_target="tpu_custom_call" | custom-call | tf_op jit(solution)/shard_map/force_smooth/pallas_call | solution.py:412
  70.4 1.8 %multiply_subtract_fusion = f32[16,16,256]{2,1,0:T(8,128)} fusion(f32[16,16,256]{2,1,0:T(8,128)} %param.9, f32[16,16,256]{2,1,0:T(8,128)} %force_smooth.1), kind=kLoop, calls=%fused_computation | loop fusion | flops 262144 | bytes 786432 | tf_op jit(solution)/shard_map/sub | solution.py:444

commit v3 on v2

--- a/solution.py
+++ b/solution.py
@@ -12,28 +12,26 @@
 
 N = 256
 RING = 8
+ZG = 4
+XG = 2
+ZP, XP = 16 // ZG, 16 // XG
 f32 = jnp.float32
 bf16 = jnp.bfloat16
 MESH = pl.DeviceIdType.MESH
 
 
 ORDER = (
-    ("zx", 0, 0, 0), ("zx", 0, 0, 1), ("zx", 0, 1, 0), ("zx", 0, 1, 1), ("zx", 0, 2, 0), ("zx", 0, 2, 1),
-    ("xp", 0, 0, 0), ("xp", 1, 1, 0), ("xp", 0, 1, 0), ("xp", 0, 2, 0), ("zx", 1, 0, 0), ("zx", 1, 0, 1),
-    ("zx", 0, 3, 0), ("zx", 1, 1, 1), ("xp", 2, 3, 0), ("xp", 0, 3, 0), ("xz", 0, 0, 0), ("xp", 2, 2, 0),
-    ("xp", 4, 2, 0), ("xp", 1, 0, 0), ("xp", 1, 2, 0), ("zx", 0, 3, 1), ("zx", 1, 1, 0), ("xp", 1, 3, 0),
-    ("xp", 7, 2, 0), ("xz", 0, 1, 1), ("xp", 2, 0, 0), ("xp", 4, 0, 0), ("zx", 1, 2, 0), ("xp", 4, 3, 0),
-    ("zx", 2, 0, 0), ("xp", 7, 0, 0), ("zx", 1, 2, 1), ("xp", 2, 1, 0), ("xz", 0, 2, 0), ("xp", 6, 2, 0),
-    ("xz", 0, 3, 1), ("xz", 0, 2, 1), ("zx", 2, 1, 1), ("xp", 6, 1, 0), ("zx", 1, 3, 1), ("xz", 1, 0, 0),
-    ("xp", 3, 0, 0), ("xp", 3, 2, 0), ("zx", 1, 3, 0), ("zx", 2, 2, 0), ("xz", 0, 3, 0), ("zx", 2, 2, 1),
-    ("xz", 1, 2, 0), ("xz", 1, 3, 1), ("xp", 5, 2, 0), ("zx", 3, 0, 0), ("zx", 2, 1, 0), ("xp", 3, 3, 0),
-    ("xz", 0, 0, 1), ("zx", 3, 1, 1), ("xz", 0, 1, 0), ("xp", 4, 1, 0), ("xp", 3, 1, 0), ("xp", 5, 1, 0),
-    ("xz", 1, 1, 1), ("zx", 2, 3, 1), ("xp", 6, 3, 0), ("xp", 5, 3, 0), ("xz", 2, 0, 0), ("xz", 1, 2, 1),
-    ("xz", 2, 3, 1), ("xz", 2, 2, 0), ("xz", 1, 0, 1), ("xp", 6, 0, 0), ("xz", 1, 3, 0), ("xz", 2, 1, 1),
-    ("xp", 5, 0, 0), ("xp", 7, 3, 0), ("zx", 2, 0, 1), ("zx", 2, 3, 0), ("xp", 7, 1, 0), ("xz", 1, 1, 0),
-    ("zx", 3, 3, 1), ("zf", 0, 1, 0), ("zx", 3, 2, 0), ("xz", 3, 2, 0), ("xz", 2, 0, 1), ("xz", 3, 0, 0),
-    ("xz", 2, 3, 0), ("xz", 2, 2, 1), ("xz", 3, 3, 1), ("xz", 3, 1, 1), ("xz", 2, 1, 0), ("zf", 0, 0, 0),
-    ("zf", 0, 3, 0), ("zf", 0, 2, 0), ("xf", 0, 2, 0), ("xf", 0, 3, 0), ("xf", 0, 0, 0), ("xf", 0, 1, 0),
+    ("zx", 0, 0, 1), ("zx", 0, 0, 0), ("zx", 0, 1, 1), ("xp", 4, 0, 0), ("zx", 0, 1, 0), ("xp", 0, 0, 0),
+    ("zx", 0, 2, 1), ("zx", 0, 2, 0), ("xp", 0, 1, 0), ("zx", 0, 3, 1), ("xp", 1, 0, 0), ("zx", 0, 3, 0),
+    ("zx", 1, 0, 0), ("xp", 2, 0, 0), ("xp", 2, 1, 0), ("zx", 1, 0, 1), ("zx", 1, 2, 1), ("xz", 0, 0, 0),
+    ("zx", 1, 1, 0), ("zx", 1, 3, 1), ("xp", 1, 1, 0), ("zx", 1, 2, 0), ("xz", 0, 1, 1), ("zx", 1, 3, 0),
+    ("zx", 2, 0, 0), ("zx", 1, 1, 1), ("xp", 3, 1, 0), ("zx", 2, 2, 1), ("xp", 4, 1, 0), ("xz", 1, 0, 0),
+    ("zx", 2, 0, 1), ("zx", 2, 1, 0), ("xp", 5, 0, 0), ("zx", 2, 3, 1), ("xp", 5, 1, 0), ("xp", 6, 0, 0),
+    ("xp", 3, 0, 0), ("zx", 2, 2, 0), ("zx", 2, 3, 0), ("xz", 0, 0, 1), ("xz", 1, 1, 1), ("xz", 0, 1, 0),
+    ("zx", 3, 2, 1), ("xp", 6, 1, 0), ("xp", 7, 0, 0), ("zx", 3, 3, 1), ("xp", 7, 1, 0), ("zx", 3, 0, 0),
+    ("zx", 2, 1, 1), ("zx", 3, 1, 0), ("xz", 2, 0, 0), ("xz", 2, 1, 1), ("xz", 1, 1, 0), ("xz", 1, 0, 1),
+    ("zf", 0, 2, 0), ("zf", 0, 3, 0), ("zf", 0, 1, 0), ("zf", 0, 0, 0), ("xz", 3, 1, 1), ("xz", 3, 0, 0),
+    ("xz", 2, 0, 1), ("xz", 2, 1, 0), ("xf", 0, 0, 0), ("xf", 0, 1, 0),
 )
 
 
@@ -133,17 +131,17 @@
     def rows(start, size):
         return pl.ds(pl.multiple_of(start, 8), size)
 
-    def hops(g, d):
-        return 4 if d == g % 2 else 3
+    def hops(buf, g, d):
+        return 4 if d == 2 * g // buf.shape[2] else 3
 
     def owner(d, dist):
         return (z + dist) % RING if d == 0 else (z + RING - dist) % RING
 
     def t_zx(g, zo):
-        return T.at[pl.ds(4 * g, 4), rows(32 * zo, 16), :]
+        return T.at[pl.ds(ZP * g, ZP), rows(32 * zo, 16), :]
 
     def t_xz(g, zo, side):
-        return T.at[pl.ds(4 * g, 4), rows(32 * zo + 16 + 8 * side, 8), :]
+        return T.at[pl.ds(XP * g, XP), rows(32 * zo + 16 + 8 * side, 8), :]
 
     def piece(d, dist):
         return {4: 0, 3: 1 + d, 2: 3 + d, 1: 5 + d, 0: 7}[dist]
@@ -165,7 +163,7 @@
     xz = (xzr, xz_s, xz_r)
 
     def zx_send(g, d, r):
-        own = t_zx(g, owner(d, hops(g, d) - r))
+        own = t_zx(g, owner(d, hops(zxr, g, d) - r))
         if r == 0:
             hop(*zx, g, d, 0, own).start()
         else:
@@ -174,7 +172,7 @@
             hop(*zx, g, d, r).start()
 
     def xz_send(g, d, r):
-        dist = hops(g, d) - r
+        dist = hops(xzr, g, d) - r
         k = piece(d, dist)
         own = t_xz(g, owner(d, dist), xlo)
         xp(g, k).wait_recv()
@@ -192,20 +190,20 @@
 
     def last(buf, sems_s, sems_r, g):
         for d in range(2):
-            arrived(buf, sems_s, sems_r, g, d, hops(g, d) - 1)
-        return buf[0, hops(g, 0) - 1, g] + buf[1, hops(g, 1) - 1, g]
+            arrived(buf, sems_s, sems_r, g, d, hops(buf, g, d) - 1)
+        return buf[0, hops(buf, g, 0) - 1, g] + buf[1, hops(buf, g, 1) - 1, g]
 
     def zx_last(g):
         total = t_zx(g, z)[...] + last(*zx, g)
-        for q in range(4):
-            put(rt0.at[0], 4 * g + q, total[q, :8])
-            put(rt0.at[1], 4 * g + q, total[q, 8:])
+        for x in range(ZP):
+            put(rt0.at[0], ZP * g + x, total[x, :8])
+            put(rt0.at[1], ZP * g + x, total[x, 8:])
 
     def xz_last(g):
         xp(g, 7).wait_recv()
         total = t_xz(g, z, xlo)[...] + xpr[7, g] + last(*xz, g)
-        for q in range(4):
-            put(rt1, 4 * g + q, total[q])
+        for x in range(XP):
+            put(rt1, XP * g + x, total[x])
 
     def to_even(m):
         side, q = m // 8, (m + j // 2) % 8
@@ -271,14 +269,15 @@
     }
     computed = summed = 0
     for name, r, g, d in ORDER:
-        while computed <= g:
+        groups = ZG if name[0] == "z" else XG
+        while computed < 4 * (g + 1) // groups:
             compute(computed)
             if computed == 0:
                 pl.semaphore_wait(barrier, 45)
             computed += 1
         act[name](g, d, r)
         summed += name == "zf"
-        if name == "zf" and summed == 4:
+        if name == "zf" and summed == ZG:
             even_sends()
     odd_sends()
 
@@ -373,11 +372,13 @@
     res = dot3(halves(dr[...].reshape(N, N)), (tab[4], tab[5]), ((0,), (0,)))
     out_ref[...] = res.reshape(16, 16, N)
 
-    for g in range(4):
-        for d in range(2):
-            for r in range(hops(g, d)):
-                hop(*zx, g, d, r, zxr.at[d, r, g]).wait_send()
-                hop(*xz, g, d, r, xzr.at[d, r, g]).wait_send()
+    for one in (zx, xz):
+        buf = one[0]
+        for g in range(buf.shape[2]):
+            for d in range(2):
+                for r in range(hops(buf, g, d)):
+                    hop(*one, g, d, r, buf.at[d, r, g]).wait_send()
+    for g in range(XG):
         for k in range(8):
             xp(g, k).wait_send()
 
@@ -419,9 +420,9 @@
             pltpu.VMEM((7, N, N), bf16),
             pltpu.VMEM((N, N + 128), f32),
             pltpu.VMEM((16, N, N), f32),
-            pltpu.VMEM((2, 4, 4, 4, 16, N), f32),
-            pltpu.VMEM((2, 4, 4, 4, 8, N), f32),
-            pltpu.VMEM((8, 4, 4, 8, N), f32),
+            pltpu.VMEM((2, 4, ZG, ZP, 16, N), f32),
+            pltpu.VMEM((2, 4, XG, XP, 8, N), f32),
+            pltpu.VMEM((8, XG, XP, 8, N), f32),
             pltpu.VMEM((2, 2, 128, 128), f32),
             pltpu.VMEM((2, 128, 128), f32),
             pltpu.VMEM((2, 2, N, 128), f32),
@@ -429,13 +430,13 @@
             pltpu.VMEM((2, 16, 8, N), f32),
             pltpu.VMEM((2, 16, 8, N), f32),
             dma((4, 3)), dma, dma,
-            dma((2, 4, 4)), dma((2, 4, 4)), dma((2, 4, 4)), dma((2, 4, 4)),
-            dma((8, 4)), dma((8, 4)),
+            dma((2, 4, ZG)), dma((2, 4, ZG)), dma((2, 4, XG)), dma((2, 4, XG)),
+            dma((8, XG)), dma((8, XG)),
             dma((2, 8)), dma((8,)), dma((2, 16)),
             dma((16,)), dma((16,)), dma((2, 16)), dma((2, 16)),
         ],
         compiler_params=pltpu.CompilerParams(
-            collective_id=0, has_side_effects=True, vmem_limit_bytes=67043328
+            collective_id=0, has_side_effects=True, vmem_limit_bytes=(65536 - 10752) << 10
         ),
         name="force_smooth",
     )(

time: 72.5 us -> 69.7 us (0.961)
  Pallas kernels: 70.4 us -> 68.8 us
  other arithmetic: 1.78 us -> 0.75 us
    pallas_call x1, Pallas kernels: 70.4 us -> 68.8 us  [body(): pl.pallas_call(kernel, out_shape=jax.ShapeDtypeStruct((16, 16, N), f32),...]
    sub x1, other arithmetic: 1.78 us -> 0.75 us  [body(): return velocity - step_size * (2.0 * velocity - smoothed)]
where the time goes in v3:
time: 69.7 us; the launch traced here: 69.6 us
  Pallas kernels  68.8 us (99%)
  other arithmetic  0.75 us (1%)
    pallas_call x1, Pallas kernels, body(): pl.pallas_call(kernel, out_shape=jax.ShapeDtypeStruct((16, 16, N), f32),...  68.8 us

profile of v3, /device:TPU:2, one launch (start us, length us, event | category | flops | bytes accessed | tf_op | source)
XLA Modules:
  0.0 69.6 jit_solution(14350871617992445992)
XLA Ops:
  0.0 0.0 copy-start
  0.0 68.8 %force_smooth.1 = f32[16,16,256]{2,1,0:T(8,128)S(1)} custom-call(bf16[2,16,256,256]{3,2,1,0:T(8,128)(2,1)} %w_hbm.1, bf16[2,16,256,256]{3,2,1,0:T(8,128)(2,1)} %i_hbm.1, bf16[2,16,256,256]{3,2,1,0:T(8,128)(2,1)} %j_hbm.1, bf16[7,256,256]{2,1,0:T(8,128)(2,1)} %constant.8.clone.tab_hbm, f32[256,384]{1,0:T(8,128)} %constant.9.clone.damp_hbm), custom_call_target="tpu_custom_call" | custom-call | tf_op jit(solution)/shard_map/force_smooth/pallas_call | solution.py:413
  68.8 0.0 copy-done
  68.9 0.8 %multiply_subtract_fusion = f32[16,16,256]{2,1,0:T(8,128)} fusion(f32[16,16,256]{2,1,0:T(8,128)S(1)} %copy-done, f32[16,16,256]{2,1,0:T(8,128)S(1)} %force_smooth.1), kind=kLoop, calls=%fused_computation | loop fusion | flops 262144 | bytes 786432 | tf_op jit(solution)/shard_map/sub | solution.py:445
Async XLA Ops:
  0.0 68.8 %copy-start = (f32[16,16,256]{2,1,0:T(8,128)S(1)}, f32[16,16,256]{2,1,0:T(8,128)}, u32[]{:S(2)}) copy-start(f32[16,16,256]{2,1,0:T(8,128)} %param.9) | copy-start | bytes 786436

commit v4 on v3

--- a/solution.py
+++ b/solution.py
@@ -362,14 +362,17 @@
 
         dr[half, s] = ws[half, s]
 
-    @pl.loop(1, 16)
-    def _(i):
-        src = (s + i) % 16
-        for half in range(2):
+    res = None
+    for half in range(2):
+        @pl.loop(1, 16)
+        def _(i):
+            src = (s + i) % 16
             part = dr.at[half, src]
             remote(part, part, d_s.at[half, src], d_r.at[half, src], src, j).wait_recv()
 
-    res = dot3(halves(dr[...].reshape(N, N)), (tab[4], tab[5]), ((0,), (0,)))
+        k = slice(128 * half, 128 * half + 128)
+        term = dot3(halves(dr[half].reshape(128, N)), (tab[4, k], tab[5, k]), ((0,), (0,)))
+        res = term if res is None else res + term
     out_ref[...] = res.reshape(16, 16, N)
 
     for one in (zx, xz):

time: 69.7 us -> 69.7 us (level)
  no operation moved by 1% of the time
where the time goes in v4:
time: 69.7 us; the launch traced here: 69.6 us
  Pallas kernels  68.9 us (99%)
  other arithmetic  0.75 us (1%)
    pallas_call x1, Pallas kernels, body(): pl.pallas_call(kernel, out_shape=jax.ShapeDtypeStruct((16, 16, N), f32),...  68.9 us

profile of v4, /device:TPU:2, one launch (start us, length us, event | category | flops | bytes accessed | tf_op | source)
XLA Modules:
  0.0 69.6 jit_solution(2848053160454325220)
XLA Ops:
  0.0 0.0 copy-start
  0.0 68.9 %force_smooth.1 = f32[16,16,256]{2,1,0:T(8,128)S(1)} custom-call(bf16[2,16,256,256]{3,2,1,0:T(8,128)(2,1)} %w_hbm.1, bf16[2,16,256,256]{3,2,1,0:T(8,128)(2,1)} %i_hbm.1, bf16[2,16,256,256]{3,2,1,0:T(8,128)(2,1)} %j_hbm.1, bf16[7,256,256]{2,1,0:T(8,128)(2,1)} %constant.8.clone.tab_hbm, f32[256,384]{1,0:T(8,128)} %constant.9.clone.damp_hbm), custom_call_target="tpu_custom_call" | custom-call | tf_op jit(solution)/shard_map/force_smooth/pallas_call | solution.py:416
  68.9 0.0 copy-done
  68.9 0.8 %multiply_subtract_fusion = f32[16,16,256]{2,1,0:T(8,128)} fusion(f32[16,16,256]{2,1,0:T(8,128)S(1)} %copy-done, f32[16,16,256]{2,1,0:T(8,128)S(1)} %force_smooth.1), kind=kLoop, calls=%fused_computation | loop fusion | flops 262144 | bytes 786432 | tf_op jit(solution)/shard_map/sub | solution.py:448
Async XLA Ops:
  0.0 68.9 %copy-start = (f32[16,16,256]{2,1,0:T(8,128)S(1)}, f32[16,16,256]{2,1,0:T(8,128)}, u32[]{:S(2)}) copy-start(f32[16,16,256]{2,1,0:T(8,128)} %param.9) | copy-start | bytes 786436
